TPU v7x, 32 devices: a whole 2x2x4 slice. The times are simulated.
32 devices in a mesh: row: 4 (over z), col: 8 (over y, x, core).
Axes of the slice: x: 2, y: 2, z: 4, core: 2. Of those that a mesh axis runs over, the one named last changes fastest.
Arguments:
- top_in: bfloat16 [8, 96, 1920], P('col'), may hold values from -6 to 6
- bottom_in: bfloat16 [8, 96, 1920], P('col'), may hold values from -6 to 6
- row_tensor: bfloat16 [4, 8, 20, 20, 400], P('row', 'col'), may hold values from -0.3125 to 0.3125
- left_proj: bfloat16 [2, 4, 8, 96, 1920], P(None, 'row', 'col'), may hold values from -0.125 to 0.125
- right_proj: bfloat16 [2, 4, 8, 96, 1920], P(None, 'row', 'col'), may hold values from -0.125 to 0.125
Outputs:
- env: bfloat16 [2, 4, 8, 96, 1920], P(None, 'row', 'col')
All inputs are finite; a program needn't handle non-finite values.
Results may differ from a plain program's by a relative error of at most 0.014.
Values may be sent and summed in bfloat16 or wider, within the bound.
A program may use at most 128 MiB of HBM per device.

v0:
```python
import functools

import jax
import jax.numpy as jnp
from jax import lax
from jax.experimental import pallas as pl
from jax.experimental.pallas import tpu as pltpu
from jax.sharding import PartitionSpec as P

epsilon = 1e-06
LANES = 128
CHUNK = 16


def round_up(value, unit):
    return -(-value // unit) * unit


def absorb_kernel(chi, pair, padded, chunk, role, held_ref, left_ref, site_ref, right_ref, out_ref,
                  wide, right_wide, first, spread, turned, grown, total):
    step = pl.program_id(0)
    active = role[0] == 1

    @pl.when(active & (step == 0))
    def _():
        total[...] = jnp.zeros_like(total)
        wide[...] = jnp.zeros_like(wide)
        right_wide[...] = jnp.zeros_like(right_wide)
        for leg in range(pair):
            wide[:, leg * LANES:leg * LANES + chi] = held_ref[:, leg * chi:(leg + 1) * chi]
            right_wide[leg * LANES:leg * LANES + chi, :chi] = right_ref[0, :, leg * chi:(leg + 1) * chi]

    @pl.when(active)
    def _():
        for duo in range(pair // 2):
            part = jnp.dot(
                left_ref[0], wide[:, duo * 2 * LANES:(duo + 1) * 2 * LANES],
                preferred_element_type=jnp.float32,
            )
            for bond in range(chunk):
                rows = part[bond * padded:(bond + 1) * padded]
                both = jnp.concatenate([rows[:, :LANES], rows[:, LANES:]], axis=0)
                first[duo * 2 * padded:(duo + 1) * 2 * padded, bond * LANES:(bond + 1) * LANES] = both.astype(jnp.bfloat16)
        for duo in range(chunk // 2):
            second = jnp.dot(
                site_ref[0], first[:, duo * 2 * LANES:(duo + 1) * 2 * LANES],
                preferred_element_type=jnp.float32,
            )
            for leg in range(pair):
                rows = second[leg * padded:(leg + 1) * padded]
                both = jnp.concatenate([rows[:, :LANES], rows[:, LANES:]], axis=0)
                spread[duo * 2 * padded:(duo + 1) * 2 * padded, leg * LANES:(leg + 1) * LANES] = both.astype(jnp.bfloat16)
        done = jnp.dot(spread[...], right_wide[...], preferred_element_type=jnp.float32)
        total[...] += jnp.sum((done * done).reshape(-1, 8, LANES), axis=0)
        turned[...] = done
        at = pl.multiple_of(step * chunk, chunk)
        for leg in range(pair):
            rows = turned[pl.ds(leg, chunk, stride=padded), :]
            grown[pl.ds(at, chunk), leg * chi:(leg + 1) * chi] = rows[:, :chi]

    @pl.when(active & (step == pl.num_programs(0) - 1))
    def _():
        mean = jnp.sum(total[...]) / (chi * pair * chi)
        factor = lax.rsqrt(jnp.full((1, 1), mean + epsilon, jnp.float32))
        out_ref[...] = (grown[...] * factor).astype(jnp.bfloat16)


def absorb(role, held, left, site, right, chi, pair, padded):
    chunk = CHUNK
    return pl.pallas_call(
        functools.partial(absorb_kernel, chi, pair, padded, chunk),
        out_shape=jax.ShapeDtypeStruct(held.shape, held.dtype),
        grid_spec=pltpu.PrefetchScalarGridSpec(
            num_scalar_prefetch=1,
            grid=(chi // chunk,),
            in_specs=[
                pl.BlockSpec(held.shape, lambda s, role: (0, 0)),
                pl.BlockSpec((1, chunk * padded, chi), lambda s, role: (role[1], s, 0)),
                pl.BlockSpec((1,) + site.shape[1:], lambda s, role: (role[1], 0, 0)),
                pl.BlockSpec((1,) + right.shape[1:], lambda s, role: (role[1], 0, 0)),
            ],
            out_specs=pl.BlockSpec(held.shape, lambda s, role: (0, 0)),
            scratch_shapes=[
                pltpu.VMEM((chi, pair * LANES), jnp.bfloat16),
                pltpu.VMEM((pair * LANES, LANES), jnp.bfloat16),
                pltpu.VMEM((pair * padded, chunk * LANES), jnp.bfloat16),
                pltpu.VMEM((chunk * padded, pair * LANES), jnp.bfloat16),
                pltpu.VMEM((chunk * padded, LANES), jnp.float32),
                pltpu.VMEM(held.shape, jnp.float32),
                pltpu.VMEM((8, LANES), jnp.float32),
            ],
        ),
        name="absorb",
    )(role, held, left, site, right)


def local(top_in, bottom_in, row_tensor, left_proj, right_proj):
    row_count = lax.axis_size("row")
    col_count = lax.axis_size("col")
    row_index = lax.axis_index("row")
    chi = top_in.shape[1]
    pair = row_tensor.shape[2]
    padded = round_up(pair, 8)
    extra = padded - pair

    ring = [(source, (source + 1) % col_count) for source in range(col_count)]
    incoming = lax.ppermute(left_proj[:, 0, 0], "col", ring)
    left = jnp.transpose(incoming.reshape(2, chi, pair, chi), (0, 3, 2, 1))
    left = jnp.pad(left, ((0, 0), (0, 0), (0, extra), (0, 0))).reshape(2, chi * padded, chi)
    right = right_proj[:, 0, 0]
    tensor = row_tensor[0, 0].reshape(pair, pair, pair, pair)
    sites = jnp.stack([jnp.transpose(tensor, (2, 3, 1, 0)), jnp.transpose(tensor, (2, 1, 3, 0))])
    sites = jnp.pad(sites, ((0, 0), (0, 0), (0, extra), (0, 0), (0, extra)))
    sites = sites.reshape(2, pair * padded, pair * padded)

    held = jnp.where(row_index < row_count // 2, top_in[0], bottom_in[0])
    top_env = bottom_env = None
    for turn in range(row_count):
        top_turn = row_index == turn
        bottom_turn = row_index == row_count - 1 - turn
        role = jnp.stack([top_turn | bottom_turn, bottom_turn]).astype(jnp.int32)
        result = absorb(role, held, left, sites, right, chi, pair, padded)
        top_env = result if turn == 0 else jnp.where(top_turn, result, top_env)
        bottom_env = result if turn == 0 else jnp.where(bottom_turn, result, bottom_env)
        if turn + 1 < row_count:
            held = lax.ppermute(
                result, "row",
                [(turn, turn + 1), (row_count - 1 - turn, row_count - 2 - turn)],
            )
    return jnp.stack([top_env, bottom_env])[:, None, None]


def solution(mesh):
    return jax.shard_map(
        local,
        mesh=mesh,
        in_specs=(
            P("col", None, None),
            P("col", None, None),
            P("row", "col", None, None, None),
            P(None, "row", "col", None, None),
            P(None, "row", "col", None, None),
        ),
        out_specs=P(None, "row", "col", None, None),
        check_vma=False,
    )
```

profile of v0, /device:TPU:0, one launch (start us, length us, event | category | flops | bytes accessed | tf_op | source)
XLA Modules:
  0.0 171.9 jit_solution(8259500591549903620)
XLA Ops:
  0.5 3.0 %reshape_squeeze.3 = bf16[20,20,20,20]{3,2,1,0:T(8,128)(2,1)S(1)} reshape(bf16[1,1,20,20,400]{4,3,2,1,0:T(8,128)(2,1)} %param.7) | data formatting | bytes 640000 | tf_op jit(solution)/shard_map/reshape;squeeze | solution.py:111
  3.5 9.1 %copy.17 = bf16[20,20,20,20]{0,1,3,2:T(8,128)(2,1)} copy(bf16[20,20,20,20]{3,2,1,0:T(8,128)(2,1)S(1)} %reshape_squeeze.3) | data formatting | bytes 640000 | tf_op jit(solution)/shard_map/reshape;squeeze | solution.py:111
  12.7 4.1 %copy.18 = bf16[20,20,20,20]{0,3,1,2:T(8,128)(2,1)} copy(bf16[20,20,20,20]{3,2,1,0:T(8,128)(2,1)S(1)} %reshape_squeeze.3) | data formatting | bytes 640000 | tf_op jit(solution)/shard_map/reshape;squeeze | solution.py:111
  16.8 6.8 %fusion.5 = bf16[2,20,24,20,24]{4,3,2,1,0:T(8,128)(2,1)} fusion(bf16[1,20,20,20,20]{4,3,2,1,0:T(8,128)(2,1)} %bitcast.37, bf16[1,20,20,20,20]{4,3,2,1,0:T(8,128)(2,1)} %bitcast.36), kind=kLoop, calls=%fused_computation.7 | loop fusion | flops 5068800 | bytes 1561600 | tf_op jit(solution)/shard_map/stack | solution.py:112
  23.6 7.5 %reshape.13.site_ref = bf16[2,480,480]{2,1,0:T(8,128)(2,1)} reshape(bf16[2,20,24,20,24]{4,3,2,1,0:T(8,128)(2,1)} %fusion.5) | data formatting | bytes 1843200 | tf_op jit(solution)/shard_map/reshape | solution.py:114
  31.7 0.8 select_bitcast_fusion.2.held_ref
  32.5 0.6 copy.15
  33.5 1.3 pad.8.clone
  34.8 23.7 %absorb.4 = bf16[96,1920]{1,0:T(8,128)(2,1)} custom-call(s32[2]{0:T(128)} %add_convert_fusion.3.role, bf16[96,1920]{1,0:T(8,128)(2,1)} %select_bitcast_fusion.2.held_ref, bf16[2,2304,96]{2,1,0:T(8,128)(2,1)} %bitcast.28, bf16[2,480,480]{2,1,0:T(8,128)(2,1)} %reshape.13.site_ref, bf16[2,96,1920]{2,1,0:T(8,128)(2,1)} %bitcast.32), custom_call_target="tpu_custom_call" | custom-call | tf_op jit(solution)/shard_map/absorb/pallas_call | solution.py:70
  58.5 1.4 collective-permute-start.1
  60.6 6.7 %collective-permute-done.1.held_ref = bf16[96,1920]{1,0:T(8,128)(2,1)S(1)} collective-permute-done((bf16[96,1920]{1,0:T(8,128)(2,1)}, bf16[96,1920]{1,0:T(8,128)(2,1)S(1)}, u32[]{:S(2)}, u32[]{:S(2)}) %collective-permute-start.1) | collective-permute-done | bytes 368672 | tf_op jit(solution)/shard_map/ppermute | solution.py:126
  67.3 0.7 copy-done.2
  68.1 4.6 %absorb.5 = bf16[96,1920]{1,0:T(8,128)(2,1)} custom-call(s32[2]{0:T(128)} %add_convert_fusion.2.role, bf16[96,1920]{1,0:T(8,128)(2,1)} %copy-done.2, bf16[2,2304,96]{2,1,0:T(8,128)(2,1)} %bitcast.29, bf16[2,480,480]{2,1,0:T(8,128)(2,1)} %reshape.13.site_ref, bf16[2,96,1920]{2,1,0:T(8,128)(2,1)} %bitcast.33), custom_call_target="tpu_custom_call" | custom-call | tf_op jit(solution)/shard_map/absorb/pallas_call | solution.py:70
  72.6 1.0 collective-permute-start.2
  73.6 0.6 add_convert_fusion.1.role
  74.3 0.7 copy-done.4
  75.0 4.6 %absorb.6 = bf16[96,1920]{1,0:T(8,128)(2,1)} custom-call(s32[2]{0:T(128)} %add_convert_fusion.1.role, bf16[96,1920]{1,0:T(8,128)(2,1)} %copy-done.4, bf16[2,2304,96]{2,1,0:T(8,128)(2,1)} %bitcast.30, bf16[2,480,480]{2,1,0:T(8,128)(2,1)} %reshape.13.site_ref, bf16[2,96,1920]{2,1,0:T(8,128)(2,1)} %bitcast.34), custom_call_target="tpu_custom_call" | custom-call | tf_op jit(solution)/shard_map/absorb/pallas_call | solution.py:70
  79.6 1.3 collective-permute-start.3
  80.8 0.6 add_convert_fusion.role
  81.5 63.8 %collective-permute-done.3.held_ref = bf16[96,1920]{1,0:T(8,128)(2,1)S(1)} collective-permute-done((bf16[96,1920]{1,0:T(8,128)(2,1)}, bf16[96,1920]{1,0:T(8,128)(2,1)S(1)}, u32[]{:S(2)}, u32[]{:S(2)}) %collective-permute-start.3) | collective-permute-done | bytes 368672 | tf_op jit(solution)/shard_map/ppermute | solution.py:126
  145.3 0.7 copy-done.3
  146.0 23.7 %absorb.7 = bf16[96,1920]{1,0:T(8,128)(2,1)} custom-call(s32[2]{0:T(128)} %add_convert_fusion.role, bf16[96,1920]{1,0:T(8,128)(2,1)} %copy-done.3, bf16[2,2304,96]{2,1,0:T(8,128)(2,1)} %bitcast.31, bf16[2,480,480]{2,1,0:T(8,128)(2,1)} %reshape.13.site_ref, bf16[2,96,1920]{2,1,0:T(8,128)(2,1)} %bitcast.35), custom_call_target="tpu_custom_call" | custom-call | tf_op jit(solution)/shard_map/absorb/pallas_call | solution.py:70
  169.7 1.2 select_bitcast_fusion.1
  171.0 0.9 maximum_bitcast_fusion
  (17 shorter events, 2.1 us)
Async XLA Ops:
  0.0 32.5 %collective-permute-start = (bf16[2,96,1920]{2,1,0:T(8,128)(2,1)}, bf16[2,96,1920]{2,1,0:T(8,128)(2,1)S(1)}, u32[]{:S(2)}, u32[]{:S(2)}) collective-permute-start(bf16[2,96,1920]{2,1,0:T(8,128)(2,1)} %bitcast.39), channel_id=1, source_target_pairs={{0,1},{1,2},{2,3},{3,4},{4,5},{5,6},{6,7},{7,0},{8,9},{9,10},{10,1... | collective-permute-start | bytes 2211848 | tf_op jit(solution)/shard_map/ppermute | solution.py:107
  23.6 8.1 %copy-start.5 = (bf16[1,96,1920]{2,1,0:T(8,128)(2,1)S(1)}, bf16[1,96,1920]{2,1,0:T(8,128)(2,1)}, u32[]{:S(2)}) copy-start(bf16[1,96,1920]{2,1,0:T(8,128)(2,1)} %param.5) | copy-start | bytes 1105924
  23.6 8.1 %copy-start.6 = (bf16[1,96,1920]{2,1,0:T(8,128)(2,1)S(1)}, bf16[1,96,1920]{2,1,0:T(8,128)(2,1)}, u32[]{:S(2)}) copy-start(bf16[1,96,1920]{2,1,0:T(8,128)(2,1)} %param.6) | copy-start | bytes 1105924
  58.5 111.2 %copy-start = (bf16[96,1920]{1,0:T(8,128)(2,1)S(1)}, bf16[96,1920]{1,0:T(8,128)(2,1)}, u32[]{:S(2)}) copy-start(bf16[96,1920]{1,0:T(8,128)(2,1)} %absorb.4) | copy-start | bytes 1105924
  58.5 8.8 %collective-permute-start.1 = (bf16[96,1920]{1,0:T(8,128)(2,1)}, bf16[96,1920]{1,0:T(8,128)(2,1)S(1)}, u32[]{:S(2)}, u32[]{:S(2)}) collective-permute-start(bf16[96,1920]{1,0:T(8,128)(2,1)} %absorb.4), channel_id=1, source_target_pairs={{0,8},{24,16},{1,9},{25,17},{2,10},{26,18},{3,11},{27,19},{4,12},{... | collective-permute-start | bytes 1105928 | tf_op jit(solution)/shard_map/ppermute | solution.py:126
  67.3 0.7 copy-start.2
  72.6 97.1 %copy-start.1 = (bf16[96,1920]{1,0:T(8,128)(2,1)S(1)}, bf16[96,1920]{1,0:T(8,128)(2,1)}, u32[]{:S(2)}) copy-start(bf16[96,1920]{1,0:T(8,128)(2,1)} %absorb.5) | copy-start | bytes 1105924
  72.6 1.6 collective-permute-start.2
  74.3 0.7 copy-start.4
  79.6 65.7 %collective-permute-start.3 = (bf16[96,1920]{1,0:T(8,128)(2,1)}, bf16[96,1920]{1,0:T(8,128)(2,1)S(1)}, u32[]{:S(2)}, u32[]{:S(2)}) collective-permute-start(bf16[96,1920]{1,0:T(8,128)(2,1)} %absorb.6), channel_id=1, source_target_pairs={{16,24},{8,0},{17,25},{9,1},{18,26},{10,2},{19,27},{11,3},{20,28},... | collective-permute-start | bytes 1105928 | tf_op jit(solution)/shard_map/ppermute | solution.py:126
  145.3 0.7 copy-start.3
where the time goes:
time: 173 us; the launch traced here: 172 us
  waiting for transfers between devices  70.5 us (41%)
  Pallas kernels  56.6 us (33%)
  local copies, waits for them, and re-layouts  28.3 us (16%)
  other arithmetic  12.2 us (7%)
  starting transfers between devices  4.19 us (2%)
    ppermute x3, waiting for transfers between devices, local(): lax.ppermute(result, 'row', [(turn, turn + 1), (row_count - 1 - turn, row...  70.5 us
    pallas_call x4, Pallas kernels, absorb(): pl.pallas_call(functools.partial(absorb_kernel, chi, pair, padded, chunk)...  56.6 us
    another operation x3, local copies, waits for them, and re-layouts, local(): tensor = row_tensor[0, 0].reshape(pair, pair, pair, pair)  16.3 us
    reshape x1, local copies, waits for them, and re-layouts, local(): sites = sites.reshape(2, pair * padded, pair * padded)  7.53 us
    another operation x1, other arithmetic, local(): jnp.stack([jnp.transpose(tensor, (2, 3, 1, 0)), jnp.transpose(tensor, (2,...  6.79 us
    ppermute x3, starting transfers between devices, local(): lax.ppermute(result, 'row', [(turn, turn + 1), (row_count - 1 - turn, row...  3.7 us
  transfers between devices with their start and end apart: 4, of which 2 were waited for; matrix products, arithmetic and copies ran while one was open for 20% of the time, Pallas kernels for 0%

commit v1 on v0

v1 whole, which is shorter than its diff:
```python
import functools

import jax
import jax.numpy as jnp
from jax import lax
from jax.experimental import pallas as pl
from jax.experimental.pallas import tpu as pltpu
from jax.sharding import PartitionSpec as P

epsilon = 1e-06
LANES = 128
CHUNK = 16


def round_up(value, unit):
    return -(-value // unit) * unit


def sweep_kernel(rows, chi, pair, padded, chunk, held_ref, left_ref, site_ref, right_ref, env_ref,
                 wide, left_tall, left_rows, right_wide, first, spread, turned, grown, total, stage, landed, scaling, send_sem, recv_sem):
    row = lax.axis_index("row")
    blocks = chi // chunk
    begin = jnp.where(row < rows // 2, 0, 1)

    barrier = pltpu.get_barrier_semaphore()

    @pl.when(row > 0)
    def _():
        pl.semaphore_signal(barrier, inc=1, device_id={"row": row - 1}, device_id_type=pl.DeviceIdType.MESH)

    @pl.when(row < rows - 1)
    def _():
        pl.semaphore_signal(barrier, inc=1, device_id={"row": row + 1}, device_id_type=pl.DeviceIdType.MESH)

    pl.semaphore_wait(barrier, jnp.where(row > 0, 1, 0) + jnp.where(row < rows - 1, 1, 0))

    wide[...] = jnp.zeros_like(wide)
    right_wide[...] = jnp.zeros_like(right_wide)
    left_tall[...] = jnp.zeros_like(left_tall)

    def prepare(which):
        for leg in range(pair):
            right_wide[which, leg * LANES:leg * LANES + chi, :chi] = right_ref[which, :, leg * chi:(leg + 1) * chi]
            piece = left_ref[which, :, leg * chi:(leg + 1) * chi].astype(jnp.float32)
            left_tall[pl.ds(leg, chi, stride=padded), :chi] = piece.T
        left_rows[which] = left_tall[...].astype(jnp.bfloat16)

    def copy_of(which, block):
        at = pl.multiple_of(block * chunk, chunk)
        return pltpu.make_async_remote_copy(
            src_ref=stage.at[which, pl.ds(at, chunk)],
            dst_ref=landed.at[which, pl.ds(at, chunk)],
            send_sem=send_sem.at[which, block],
            recv_sem=recv_sem.at[which, block],
            device_id={"row": jnp.where(which == 0, row + 1, row - 1)},
            device_id_type=pl.DeviceIdType.MESH,
        )

    def inverse_norm(square_sum):
        return lax.rsqrt(jnp.full((1, 1), jnp.sum(square_sum) / (chi * pair * chi) + epsilon, jnp.float32))

    def absorb(which, sends):
        total[...] = jnp.zeros_like(total)

        def one_block(block, carry):
            at = pl.multiple_of(block * chunk, chunk)
            left_here = left_rows[which, pl.ds(pl.multiple_of(block * chunk * padded, chunk * padded), chunk * padded), :]
            for duo in range(pair // 2):
                part = jnp.dot(
                    left_here, wide[:, duo * 2 * LANES:(duo + 1) * 2 * LANES],
                    preferred_element_type=jnp.float32,
                )
                for bond in range(chunk):
                    piece = part[bond * padded:(bond + 1) * padded]
                    both = jnp.concatenate([piece[:, :LANES], piece[:, LANES:]], axis=0)
                    first[duo * 2 * padded:(duo + 1) * 2 * padded, bond * LANES:(bond + 1) * LANES] = both.astype(jnp.bfloat16)
            for duo in range(chunk // 2):
                second = jnp.dot(
                    site_ref[which], first[:, duo * 2 * LANES:(duo + 1) * 2 * LANES],
                    preferred_element_type=jnp.float32,
                )
                for leg in range(pair):
                    piece = second[leg * padded:(leg + 1) * padded]
                    both = jnp.concatenate([piece[:, :LANES], piece[:, LANES:]], axis=0)
                    spread[duo * 2 * padded:(duo + 1) * 2 * padded, leg * LANES:(leg + 1) * LANES] = both.astype(jnp.bfloat16)
            done = jnp.dot(spread[...], right_wide[which], preferred_element_type=jnp.float32) * scaling[...]
            total[...] += jnp.sum((done * done).reshape(-1, 8, LANES), axis=0)
            turned[...] = done
            for leg in range(pair):
                piece = turned[pl.ds(leg, chunk, stride=padded), :]
                grown[pl.ds(at, chunk), leg * chi:(leg + 1) * chi] = piece[:, :chi]
            stage[which, pl.ds(at, chunk), :] = grown[pl.ds(at, chunk), :].astype(jnp.bfloat16)

            @pl.when(sends & (block > 0))
            def _():
                copy_of(which, block - 1).start()

            return carry

        lax.fori_loop(0, blocks, one_block, 0)
        factor = inverse_norm(total[...])
        env_ref[which] = (grown[...] * factor).astype(jnp.bfloat16)

        @pl.when(sends)
        def _():
            copy_of(which, blocks - 1).start()

    def unpack(source):
        for leg in range(pair):
            wide[:chi, leg * LANES:leg * LANES + chi] = source[:, leg * chi:(leg + 1) * chi]

    def one_turn(turn, carry):
        which = jnp.where(row == turn, 0, 1)
        active = (row == turn) | (row == rows - 1 - turn)
        sends = turn < rows - 1

        @pl.when(turn == 0)
        def _():
            prepare(begin)

        @pl.when(active & (turn == 0))
        def _():
            unpack(held_ref[...])
            scaling[...] = jnp.ones_like(scaling)

        @pl.when(active & (turn > 0))
        def _():
            for block in range(blocks):
                copy_of(which, block).wait_recv()
            unpack(landed[which])
            values = landed[which].astype(jnp.float32)
            scaling[...] = jnp.broadcast_to(inverse_norm(values * values), scaling.shape)

        @pl.when(active)
        def _():
            absorb(which, sends)

        @pl.when(turn == 0)
        def _():
            prepare(1 - begin)

        @pl.when(active & sends)
        def _():
            for block in range(blocks):
                copy_of(which, block).wait_send()

        return carry

    lax.fori_loop(0, rows, one_turn, 0)


def sweep(rows, held, left, site, right, chi, pair, padded):
    chunk = CHUNK
    blocks = chi // chunk
    return pl.pallas_call(
        functools.partial(sweep_kernel, rows, chi, pair, padded, chunk),
        out_shape=jax.ShapeDtypeStruct((2,) + held.shape, held.dtype),
        in_specs=[pl.BlockSpec(memory_space=pltpu.VMEM)] * 4,
        out_specs=pl.BlockSpec(memory_space=pltpu.VMEM),
        scratch_shapes=[
            pltpu.VMEM((LANES, pair * LANES), jnp.bfloat16),
            pltpu.VMEM((chi * padded, LANES), jnp.float32),
            pltpu.VMEM((2, chi * padded, LANES), jnp.bfloat16),
            pltpu.VMEM((2, pair * LANES, LANES), jnp.bfloat16),
            pltpu.VMEM((pair * padded, chunk * LANES), jnp.bfloat16),
            pltpu.VMEM((chunk * padded, pair * LANES), jnp.bfloat16),
            pltpu.VMEM((chunk * padded, LANES), jnp.float32),
            pltpu.VMEM(held.shape, jnp.float32),
            pltpu.VMEM((8, LANES), jnp.float32),
            pltpu.VMEM((2,) + held.shape, jnp.bfloat16),
            pltpu.VMEM((2,) + held.shape, jnp.bfloat16),
            pltpu.VMEM((1, LANES), jnp.float32),
            pltpu.SemaphoreType.DMA((2, blocks)),
            pltpu.SemaphoreType.DMA((2, blocks)),
        ],
        compiler_params=pltpu.CompilerParams(collective_id=0, has_side_effects=True, vmem_limit_bytes=56 * 1024 * 1024),
        name="sweep",
    )(held, left, site, right)


def local(top_in, bottom_in, row_tensor, left_proj, right_proj):
    row_count = lax.axis_size("row")
    col_count = lax.axis_size("col")
    row_index = lax.axis_index("row")
    chi = top_in.shape[1]
    pair = row_tensor.shape[2]
    padded = round_up(pair, 8)
    extra = padded - pair

    ring = [(source, (source + 1) % col_count) for source in range(col_count)]
    left = lax.ppermute(left_proj[:, 0, 0], "col", ring)
    right = right_proj[:, 0, 0]
    tensor = row_tensor[0, 0].reshape(pair, pair, pair, pair)
    sites = jnp.stack([jnp.transpose(tensor, (2, 3, 1, 0)), jnp.transpose(tensor, (2, 1, 3, 0))])
    sites = jnp.pad(sites, ((0, 0), (0, 0), (0, extra), (0, 0), (0, extra)))
    sites = sites.reshape(2, pair * padded, pair * padded)

    held = jnp.where(row_index < row_count // 2, top_in[0], bottom_in[0])
    env = sweep(row_count, held, left, sites, right, chi, pair, padded)
    return env[:, None, None]


def solution(mesh):
    return jax.shard_map(
        local,
        mesh=mesh,
        in_specs=(
            P("col", None, None),
            P("col", None, None),
            P("row", "col", None, None, None),
            P(None, "row", "col", None, None),
            P(None, "row", "col", None, None),
        ),
        out_specs=P(None, "row", "col", None, None),
        check_vma=False,
    )
```

time: 173 us -> 137 us (0.79)
  waiting for transfers between devices: 70.5 us -> 0.01 us
  Pallas kernels: 56.6 us -> 102 us
  other arithmetic: 12.2 us -> 7.6 us
  starting transfers between devices: 4.19 us -> 0.49 us
    ppermute x4 -> x1, waiting for transfers between devices: 70.5 us -> 0.01 us  [local(): left = lax.ppermute(left_proj[:, 0, 0], 'col', ring)]
    pallas_call x4 -> x1, Pallas kernels: 56.6 us -> 102 us  [sweep(): pl.pallas_call(functools.partial(sweep_kernel, rows, chi, pair, padded, c...]
    ppermute x4 -> x1, starting transfers between devices: 4.19 us -> 0.49 us  [local(): left = lax.ppermute(left_proj[:, 0, 0], 'col', ring)]
    convert_element_type x4 -> x0, other arithmetic: 2.42 us -> none  [local(): role = jnp.stack([top_turn | bottom_turn, bottom_turn]).astype(jnp.int32)]
  transfers between devices with their start and end apart: 4 -> 1, of which waited for: 2 -> 0; matrix products, arithmetic and copies ran while one was open for 20% -> 23% of each run, Pallas kernels for 0% -> 0%
where the time goes in v1:
time: 137 us
  Pallas kernels  102 us (74%)
  local copies, waits for them, and re-layouts  26.6 us (19%)
  other arithmetic  7.6 us (6%)
    pallas_call x1, Pallas kernels, sweep(): pl.pallas_call(functools.partial(sweep_kernel, rows, chi, pair, padded, c...  102 us
    another operation x3, local copies, waits for them, and re-layouts, local(): tensor = row_tensor[0, 0].reshape(pair, pair, pair, pair)  16.2 us
    reshape x1, local copies, waits for them, and re-layouts, local(): sites = sites.reshape(2, pair * padded, pair * padded)  7.53 us
    another operation x1, other arithmetic, local(): jnp.stack([jnp.transpose(tensor, (2, 3, 1, 0)), jnp.transpose(tensor, (2,...  6.8 us
    unnamed x7, local copies, waits for them, and re-layouts  2.9 us
  transfers between devices with their start and end apart: 1, of which 0 were waited for; matrix products, arithmetic and copies ran while one was open for 23% of the time, Pallas kernels for 0%

profile of v1, /device:TPU:0, one launch (start us, length us, event | category | flops | bytes accessed | tf_op | source)
XLA Modules:
  0.0 136.6 jit_solution(272764105855921604)
XLA Ops:
  0.0 0.5 collective-permute-start
  0.5 3.0 %reshape_squeeze.3 = bf16[20,20,20,20]{3,2,1,0:T(8,128)(2,1)S(1)} reshape(bf16[1,1,20,20,400]{4,3,2,1,0:T(8,128)(2,1)} %param.7) | data formatting | bytes 640000 | tf_op jit(solution)/shard_map/reshape;squeeze | solution.py:193
  3.5 9.1 %copy.9 = bf16[20,20,20,20]{0,1,3,2:T(8,128)(2,1)} copy(bf16[20,20,20,20]{3,2,1,0:T(8,128)(2,1)S(1)} %reshape_squeeze.3) | data formatting | bytes 640000 | tf_op jit(solution)/shard_map/reshape;squeeze | solution.py:193
  12.7 4.0 %copy.10 = bf16[20,20,20,20]{0,3,1,2:T(8,128)(2,1)} copy(bf16[20,20,20,20]{3,2,1,0:T(8,128)(2,1)S(1)} %reshape_squeeze.3) | data formatting | bytes 640000 | tf_op jit(solution)/shard_map/reshape;squeeze | solution.py:193
  16.7 6.8 %fusion.5 = bf16[2,20,24,20,24]{4,3,2,1,0:T(8,128)(2,1)} fusion(bf16[1,20,20,20,20]{4,3,2,1,0:T(8,128)(2,1)} %bitcast.14, bf16[1,20,20,20,20]{4,3,2,1,0:T(8,128)(2,1)} %bitcast.13), kind=kLoop, calls=%fused_computation.7 | loop fusion | flops 5068800 | bytes 1561600 | tf_op jit(solution)/shard_map/stack | solution.py:194
  23.5 0.0 copy-start.1
  23.5 0.0 copy-start.2
  23.5 7.5 %reshape.5.site_ref = bf16[2,480,480]{2,1,0:T(8,128)(2,1)} reshape(bf16[2,20,24,20,24]{4,3,2,1,0:T(8,128)(2,1)} %fusion.5) | data formatting | bytes 1843200 | tf_op jit(solution)/shard_map/reshape | solution.py:196
  31.0 0.0 copy-done.1
  31.0 0.0 copy-done.2
  31.0 0.8 select_bitcast_fusion.held_ref
  31.8 0.0 collective-permute-done.left_ref
  31.8 0.0 copy-start
  31.8 0.9 copy-done
  32.7 101.9 %sweep.1 = bf16[2,96,1920]{2,1,0:T(8,128)(2,1)} custom-call(bf16[96,1920]{1,0:T(8,128)(2,1)} %select_bitcast_fusion.held_ref, bf16[2,96,1920]{2,1,0:T(8,128)(2,1)} %copy-done, bf16[2,480,480]{2,1,0:T(8,128)(2,1)} %reshape.5.site_ref, bf16[2,96,1920]{2,1,0:T(8,128)(2,1)} %bitcast.16), custom_call_target="tpu_custom_call" | custom-call | tf_op jit(solution)/shard_map/sweep/pallas_call | solution.py:155
  134.6 2.0 %copy.13 = bf16[2,1,1,96,1920]{4,3,2,1,0:T(8,128)(2,1)} copy(bf16[2,1,1,96,1920]{4,3,2,1,0:T(8,128)(2,1)} %bitcast.15) | data formatting | bytes 1474560
Async XLA Ops:
  0.0 31.8 %collective-permute-start = (bf16[2,96,1920]{2,1,0:T(8,128)(2,1)}, bf16[2,96,1920]{2,1,0:T(8,128)(2,1)S(1)}, u32[]{:S(2)}, u32[]{:S(2)}) collective-permute-start(bf16[2,96,1920]{2,1,0:T(8,128)(2,1)} %bitcast.17), channel_id=1, source_target_pairs={{0,1},{1,2},{2,3},{3,4},{4,5},{5,6},{6,7},{7,0},{8,9},{9,10},{10,1... | collective-permute-start | bytes 2211848 | tf_op jit(solution)/shard_map/ppermute | solution.py:191
  23.5 7.5 %copy-start.1 = (bf16[1,96,1920]{2,1,0:T(8,128)(2,1)S(1)}, bf16[1,96,1920]{2,1,0:T(8,128)(2,1)}, u32[]{:S(2)}) copy-start(bf16[1,96,1920]{2,1,0:T(8,128)(2,1)} %param.5) | copy-start | bytes 1105924
  23.5 7.5 %copy-start.2 = (bf16[1,96,1920]{2,1,0:T(8,128)(2,1)S(1)}, bf16[1,96,1920]{2,1,0:T(8,128)(2,1)}, u32[]{:S(2)}) copy-start(bf16[1,96,1920]{2,1,0:T(8,128)(2,1)} %param.6) | copy-start | bytes 1105924
  31.8 0.9 copy-start

commit v2 on v1

--- a/solution.py
+++ b/solution.py
@@ -149,6 +149,61 @@
     lax.fori_loop(0, rows, one_turn, 0)
 
 
+def arrange_kernel(pair, padded, tensor_ref, site_ref, tall, turned, pieces):
+    width = pair * padded
+    slabs = tall.shape[0]
+    tall[...] = jnp.zeros_like(tall)
+    pieces[...] = jnp.zeros_like(pieces)
+    for leg in range(pair):
+        plane = tensor_ref[leg].astype(jnp.float32)
+        for slab in range(slabs):
+            part = plane[:, slab * LANES:(slab + 1) * LANES]
+            part = jnp.pad(part, ((0, 0), (0, LANES - part.shape[1])))
+            tall[slab, pl.ds(leg, pair, stride=padded), :] = part
+    for slab in range(slabs):
+        for other in range(slabs):
+            block = tall[slab, other * LANES:(other + 1) * LANES, :]
+            turned[other, slab * LANES:(slab + 1) * LANES, :] = block.T
+    gap = jnp.zeros((padded - pair, LANES), jnp.float32)
+    for slab in range(slabs):
+        lanes = min(LANES, width - slab * LANES)
+        for duo in range(pair // 2):
+            at = duo * 2 * pair
+            rows = jnp.concatenate(
+                [turned[slab, at:at + pair, :], gap, turned[slab, at + pair:at + 2 * pair, :], gap], axis=0
+            )
+            site_ref[0, duo * 2 * padded:(duo + 1) * 2 * padded, slab * LANES:slab * LANES + lanes] = (
+                rows[:, :lanes].astype(jnp.bfloat16)
+            )
+    for low in range(pair):
+        rows = jnp.concatenate(
+            [turned[slab, pl.ds(low, pair, stride=pair), :] for slab in range(slabs)], axis=1
+        )
+        for high in range(pair):
+            pieces[high, :pair, low * padded:(low + 1) * padded] = rows[:, high * padded:(high + 1) * padded]
+    tall[...] = jnp.zeros_like(tall)
+    for slab in range(slabs):
+        lanes = min(LANES, width - slab * LANES)
+        for high in range(pair):
+            tall[slab, pl.ds(high, pair, stride=padded), :] = pieces[high, :pair, slab * LANES:(slab + 1) * LANES]
+        site_ref[1, :, slab * LANES:slab * LANES + lanes] = tall[slab, :width, :lanes].astype(jnp.bfloat16)
+
+
+def arrange(tensor, pair, padded):
+    width = pair * padded
+    slabs = round_up(width, LANES) // LANES
+    return pl.pallas_call(
+        functools.partial(arrange_kernel, pair, padded),
+        out_shape=jax.ShapeDtypeStruct((2, width, width), tensor.dtype),
+        scratch_shapes=[
+            pltpu.VMEM((slabs, slabs * LANES, LANES), jnp.float32),
+            pltpu.VMEM((slabs, slabs * LANES, LANES), jnp.float32),
+            pltpu.VMEM((pair, padded, slabs * LANES), jnp.float32),
+        ],
+        name="arrange",
+    )(tensor)
+
+
 def sweep(rows, held, left, site, right, chi, pair, padded):
     chunk = CHUNK
     blocks = chi // chunk
@@ -185,15 +240,11 @@
     chi = top_in.shape[1]
     pair = row_tensor.shape[2]
     padded = round_up(pair, 8)
-    extra = padded - pair
 
     ring = [(source, (source + 1) % col_count) for source in range(col_count)]
     left = lax.ppermute(left_proj[:, 0, 0], "col", ring)
     right = right_proj[:, 0, 0]
-    tensor = row_tensor[0, 0].reshape(pair, pair, pair, pair)
-    sites = jnp.stack([jnp.transpose(tensor, (2, 3, 1, 0)), jnp.transpose(tensor, (2, 1, 3, 0))])
-    sites = jnp.pad(sites, ((0, 0), (0, 0), (0, extra), (0, 0), (0, extra)))
-    sites = sites.reshape(2, pair * padded, pair * padded)
+    sites = arrange(row_tensor[0, 0], pair, padded)
 
     held = jnp.where(row_index < row_count // 2, top_in[0], bottom_in[0])
     env = sweep(row_count, held, left, sites, right, chi, pair, padded)

time: 137 us -> 115 us (0.84)
  local copies, waits for them, and re-layouts: 26.6 us -> 2.9 us
  waiting for transfers between devices: 0.01 us -> 7.2 us
  other arithmetic: 7.6 us -> 0.79 us
  Pallas kernels: 102 us -> 104 us
    another operation x3 -> x0, local copies, waits for them, and re-layouts: 16.2 us -> none  [local(): tensor = row_tensor[0, 0].reshape(pair, pair, pair, pair)]
    reshape x1 -> x0, local copies, waits for them, and re-layouts: 7.53 us -> none  [local(): sites = sites.reshape(2, pair * padded, pair * padded)]
    ppermute x1, waiting for transfers between devices: 0.01 us -> 7.2 us  [local(): left = lax.ppermute(left_proj[:, 0, 0], 'col', ring)]
    another operation x1 -> x0, other arithmetic: 6.8 us -> none  [local(): jnp.stack([jnp.transpose(tensor, (2, 3, 1, 0)), jnp.transpose(tensor, (2,...]
    pallas_call x0 -> x1, Pallas kernels: none -> 4.22 us  [arrange(): pl.pallas_call(functools.partial(arrange_kernel, pair, padded), out_shape...]
    pallas_call x1, Pallas kernels: 102 us -> 99.4 us  [sweep(): pl.pallas_call(functools.partial(sweep_kernel, rows, chi, pair, padded, c...]
  transfers between devices with their start and end apart: 1 -> 1, of which waited for: 0 -> 1; matrix products, arithmetic and copies ran while one was open for 23% -> 1% of each run, Pallas kernels for 0% -> 4%
where the time goes in v2:
time: 115 us
  Pallas kernels  104 us (90%)
  waiting for transfers between devices  7.2 us (6%)
  local copies, waits for them, and re-layouts  2.9 us (3%)
    pallas_call x1, Pallas kernels, sweep(): pl.pallas_call(functools.partial(sweep_kernel, rows, chi, pair, padded, c...  99.4 us
    ppermute x1, waiting for transfers between devices, local(): left = lax.ppermute(left_proj[:, 0, 0], 'col', ring)  7.2 us
    pallas_call x1, Pallas kernels, arrange(): pl.pallas_call(functools.partial(arrange_kernel, pair, padded), out_shape...  4.22 us
    unnamed x7, local copies, waits for them, and re-layouts  2.9 us
  transfers between devices with their start and end apart: 1, of which 1 were waited for; matrix products, arithmetic and copies ran while one was open for 1% of the time, Pallas kernels for 4%

profile of v2, /device:TPU:0, one launch (start us, length us, event | category | flops | bytes accessed | tf_op | source)
XLA Modules:
  0.0 115.0 jit_solution(14348113495789184519)
XLA Ops:
  0.0 0.5 collective-permute-start
  0.5 0.0 copy-start.1
  0.5 0.0 copy-start.2
  0.5 4.2 %arrange.1.site_ref = bf16[2,480,480]{2,1,0:T(8,128)(2,1)} custom-call(bf16[20,20,400]{2,1,0:T(8,128)(2,1)} %bitcast.10), custom_call_target="tpu_custom_call" | custom-call | tf_op jit(solution)/shard_map/arrange/pallas_call | solution.py:195
  4.7 0.0 copy-done.1
  4.7 0.0 copy-done.2
  4.7 0.8 select_bitcast_fusion.held_ref
  5.5 7.2 %collective-permute-done.left_ref = bf16[2,96,1920]{2,1,0:T(8,128)(2,1)S(1)} collective-permute-done((bf16[2,96,1920]{2,1,0:T(8,128)(2,1)}, bf16[2,96,1920]{2,1,0:T(8,128)(2,1)S(1)}, u32[]{:S(2)}, u32[]{:S(2)}) %collective-permute-start) | collective-permute-done | bytes 737312 | tf_op jit(solution)/shard_map/ppermute | solution.py:245
  12.7 0.0 copy-start
  12.7 0.9 copy-done
  13.6 99.4 %sweep.1 = bf16[2,96,1920]{2,1,0:T(8,128)(2,1)} custom-call(bf16[96,1920]{1,0:T(8,128)(2,1)} %select_bitcast_fusion.held_ref, bf16[2,96,1920]{2,1,0:T(8,128)(2,1)} %copy-done, bf16[2,480,480]{2,1,0:T(8,128)(2,1)} %arrange.1.site_ref, bf16[2,96,1920]{2,1,0:T(8,128)(2,1)} %bitcast.9), custom_call_target="tpu_custom_call" | custom-call | tf_op jit(solution)/shard_map/sweep/pallas_call | solution.py:210
  113.0 2.0 %copy.8 = bf16[2,1,1,96,1920]{4,3,2,1,0:T(8,128)(2,1)} copy(bf16[2,1,1,96,1920]{4,3,2,1,0:T(8,128)(2,1)} %bitcast.8) | data formatting | bytes 1474560
Async XLA Ops:
  0.0 12.7 %collective-permute-start = (bf16[2,96,1920]{2,1,0:T(8,128)(2,1)}, bf16[2,96,1920]{2,1,0:T(8,128)(2,1)S(1)}, u32[]{:S(2)}, u32[]{:S(2)}) collective-permute-start(bf16[2,96,1920]{2,1,0:T(8,128)(2,1)} %bitcast.11), channel_id=1, source_target_pairs={{0,1},{1,2},{2,3},{3,4},{4,5},{5,6},{6,7},{7,0},{8,9},{9,10},{10,1... | collective-permute-start | bytes 2211848 | tf_op jit(solution)/shard_map/ppermute | solution.py:245
  0.5 4.2 %copy-start.1 = (bf16[1,96,1920]{2,1,0:T(8,128)(2,1)S(1)}, bf16[1,96,1920]{2,1,0:T(8,128)(2,1)}, u32[]{:S(2)}) copy-start(bf16[1,96,1920]{2,1,0:T(8,128)(2,1)} %param.5) | copy-start | bytes 1105924
  0.5 4.2 %copy-start.2 = (bf16[1,96,1920]{2,1,0:T(8,128)(2,1)S(1)}, bf16[1,96,1920]{2,1,0:T(8,128)(2,1)}, u32[]{:S(2)}) copy-start(bf16[1,96,1920]{2,1,0:T(8,128)(2,1)} %param.6) | copy-start | bytes 1105924
  12.7 0.9 copy-start

commit v3 on v2

--- a/solution.py
+++ b/solution.py
@@ -74,16 +74,23 @@
                     piece = part[bond * padded:(bond + 1) * padded]
                     both = jnp.concatenate([piece[:, :LANES], piece[:, LANES:]], axis=0)
                     first[duo * 2 * padded:(duo + 1) * 2 * padded, bond * LANES:(bond + 1) * LANES] = both.astype(jnp.bfloat16)
-            for duo in range(chunk // 2):
+            for quad in range(chunk // 4):
                 second = jnp.dot(
-                    site_ref[which], first[:, duo * 2 * LANES:(duo + 1) * 2 * LANES],
+                    site_ref[which], first[:, quad * 4 * LANES:(quad + 1) * 4 * LANES],
                     preferred_element_type=jnp.float32,
                 )
-                for leg in range(pair):
-                    piece = second[leg * padded:(leg + 1) * padded]
-                    both = jnp.concatenate([piece[:, :LANES], piece[:, LANES:]], axis=0)
-                    spread[duo * 2 * padded:(duo + 1) * 2 * padded, leg * LANES:(leg + 1) * LANES] = both.astype(jnp.bfloat16)
-            done = jnp.dot(spread[...], right_wide[which], preferred_element_type=jnp.float32) * scaling[...]
+                for half in range(2):
+                    duo = quad * 2 + half
+                    for leg in range(pair):
+                        piece = second[leg * padded:(leg + 1) * padded, half * 2 * LANES:(half + 1) * 2 * LANES]
+                        both = jnp.concatenate([piece[:, :LANES], piece[:, LANES:]], axis=0)
+                        spread[duo * 2 * padded:(duo + 1) * 2 * padded, leg * LANES:(leg + 1) * LANES] = both.astype(jnp.bfloat16)
+            middle = pair // 2 * LANES
+            halves = [
+                jnp.dot(spread[:, :middle], right_wide[which, :middle], preferred_element_type=jnp.float32),
+                jnp.dot(spread[:, middle:], right_wide[which, middle:], preferred_element_type=jnp.float32),
+            ]
+            done = (halves[0] + halves[1]) * scaling[...]
             total[...] += jnp.sum((done * done).reshape(-1, 8, LANES), axis=0)
             turned[...] = done
             for leg in range(pair):

time: 115 us -> 117 us (1.017)
  Pallas kernels: 104 us -> 106 us
    pallas_call x1, Pallas kernels: 99.4 us -> 101 us  [sweep(): pl.pallas_call(functools.partial(sweep_kernel, rows, chi, pair, padded, c...]
where the time goes in v3:
time: 117 us
  Pallas kernels  106 us (91%)
  waiting for transfers between devices  7.2 us (6%)
  local copies, waits for them, and re-layouts  2.9 us (2%)
    pallas_call x1, Pallas kernels, sweep(): pl.pallas_call(functools.partial(sweep_kernel, rows, chi, pair, padded, c...  101 us
    ppermute x1, waiting for transfers between devices, local(): left = lax.ppermute(left_proj[:, 0, 0], 'col', ring)  7.2 us
    pallas_call x1, Pallas kernels, arrange(): pl.pallas_call(functools.partial(arrange_kernel, pair, padded), out_shape...  4.22 us
    unnamed x7, local copies, waits for them, and re-layouts  2.9 us
  transfers between devices with their start and end apart: 1, of which 1 were waited for; matrix products, arithmetic and copies ran while one was open for 1% of the time, Pallas kernels for 4%

profile of v3, /device:TPU:0, one launch (start us, length us, event | category | flops | bytes accessed | tf_op | source)
XLA Modules:
  0.0 116.9 jit_solution(10501911030376312939)
XLA Ops:
  0.0 0.5 collective-permute-start
  0.5 0.0 copy-start.1
  0.5 0.0 copy-start.2
  0.5 4.2 %arrange.1.site_ref = bf16[2,480,480]{2,1,0:T(8,128)(2,1)} custom-call(bf16[20,20,400]{2,1,0:T(8,128)(2,1)} %bitcast.10), custom_call_target="tpu_custom_call" | custom-call | tf_op jit(solution)/shard_map/arrange/pallas_call | solution.py:202
  4.7 0.0 copy-done.1
  4.7 0.0 copy-done.2
  4.7 0.8 select_bitcast_fusion.held_ref
  5.5 7.2 %collective-permute-done.left_ref = bf16[2,96,1920]{2,1,0:T(8,128)(2,1)S(1)} collective-permute-done((bf16[2,96,1920]{2,1,0:T(8,128)(2,1)}, bf16[2,96,1920]{2,1,0:T(8,128)(2,1)S(1)}, u32[]{:S(2)}, u32[]{:S(2)}) %collective-permute-start) | collective-permute-done | bytes 737312 | tf_op jit(solution)/shard_map/ppermute | solution.py:252
  12.7 0.0 copy-start
  12.7 0.9 copy-done
  13.6 101.3 %sweep.1 = bf16[2,96,1920]{2,1,0:T(8,128)(2,1)} custom-call(bf16[96,1920]{1,0:T(8,128)(2,1)} %select_bitcast_fusion.held_ref, bf16[2,96,1920]{2,1,0:T(8,128)(2,1)} %copy-done, bf16[2,480,480]{2,1,0:T(8,128)(2,1)} %arrange.1.site_ref, bf16[2,96,1920]{2,1,0:T(8,128)(2,1)} %bitcast.9), custom_call_target="tpu_custom_call" | custom-call | tf_op jit(solution)/shard_map/sweep/pallas_call | solution.py:217
  114.9 2.0 %copy.8 = bf16[2,1,1,96,1920]{4,3,2,1,0:T(8,128)(2,1)} copy(bf16[2,1,1,96,1920]{4,3,2,1,0:T(8,128)(2,1)} %bitcast.8) | data formatting | bytes 1474560
Async XLA Ops:
  0.0 12.7 %collective-permute-start = (bf16[2,96,1920]{2,1,0:T(8,128)(2,1)}, bf16[2,96,1920]{2,1,0:T(8,128)(2,1)S(1)}, u32[]{:S(2)}, u32[]{:S(2)}) collective-permute-start(bf16[2,96,1920]{2,1,0:T(8,128)(2,1)} %bitcast.11), channel_id=1, source_target_pairs={{0,1},{1,2},{2,3},{3,4},{4,5},{5,6},{6,7},{7,0},{8,9},{9,10},{10,1... | collective-permute-start | bytes 2211848 | tf_op jit(solution)/shard_map/ppermute | solution.py:252
  0.5 4.2 %copy-start.1 = (bf16[1,96,1920]{2,1,0:T(8,128)(2,1)S(1)}, bf16[1,96,1920]{2,1,0:T(8,128)(2,1)}, u32[]{:S(2)}) copy-start(bf16[1,96,1920]{2,1,0:T(8,128)(2,1)} %param.5) | copy-start | bytes 1105924
  0.5 4.2 %copy-start.2 = (bf16[1,96,1920]{2,1,0:T(8,128)(2,1)S(1)}, bf16[1,96,1920]{2,1,0:T(8,128)(2,1)}, u32[]{:S(2)}) copy-start(bf16[1,96,1920]{2,1,0:T(8,128)(2,1)} %param.6) | copy-start | bytes 1105924
  12.7 0.9 copy-start
